TPU v7x, 256 devices: a whole 4x4x8 slice. The times are simulated.
256 devices in a mesh: dp: 4 (over x), gx: 16 (over y, z_lo, core), gy: 4 (over z_hi).
Axes of the slice: x: 4, y: 4, z: 8 (z_hi: 4, z_lo: 2; z = z_hi * 2 + z_lo), core: 2. Of those that a mesh axis runs over, the one named last changes fastest.
Arguments:
- field_in: bfloat16 [4, 32, 1024, 1024], P('dp', None, 'gx', 'gy'), parts along dimension 0, may hold values from -6 to 6
- spectral_weight: bfloat16 [32, 32, 2, 128, 128], P(None, None, None, ('gx', 'gy')), may hold values from -6 to 6
- conv_weight: bfloat16 [9, 32, 32], replicated, may hold values from -0.375 to 0.375
- conv_bias: float32 [32], replicated, may hold values from -3 to 3
- upstream: bfloat16 [4, 32, 1024, 1024], P('dp', None, 'gx', 'gy'), parts along dimension 0, may hold values from -6 to 6
Outputs:
- activation: float32 [4, 32, 1024, 1024], P('dp', None, 'gx', 'gy'), parts along dimension 0
- field_grad: float32 [4, 32, 1024, 1024], P('dp', None, 'gx', 'gy'), parts along dimension 0
- weight_grad: float32 [128, 32, 2, 128, 128], P('dp', None, None, ('gx', 'gy')), parts along dimension 0
There are 4 independent parts, one for each index of `dp`. A program takes and returns all parts, laid end to end along the dimension named above; an argument that names none is the same for every part. Nothing has to cross between parts.
All inputs are finite; a program needn't handle non-finite values.
Results may differ from a plain program's by a relative error of at most 0.02.
Values may be sent and summed in bfloat16 or wider, within the bound.
No kernel may reach another device: no remote copies, remote signals or barrier semaphores. Data moves between devices by JAX's collectives and lax.ppermute only.
A program may use at most 128 MiB of HBM per device.

v0:
```python
import math
import jax
import jax.numpy as jnp
from jax import lax
from jax.sharding import PartitionSpec as P

M1 = 128
M2 = 128


def padded_2(cells, sides, width):
    for axis, dim in sides:
        count = lax.axis_size(axis)
        ends = count - 1
        head = lax.slice_in_dim(cells, 0, width, axis=dim)
        tail = lax.slice_in_dim(cells, cells.shape[dim] - width, cells.shape[dim], axis=dim)
        cells = jnp.concatenate(
            [
                lax.ppermute(tail, axis, [(i, (i + 1) % count) for i in range(ends)]),
                cells,
                lax.ppermute(head, axis, [((i + 1) % count, i) for i in range(ends)]),
            ],
            axis=dim,
        )
    return cells


def kx_values(index, length, kept):
    return jnp.where(index < kept // 2, index, index + (length - kept))


def x_table(modes, positions, length):
    product = modes[:, None] * positions[None, :] % length
    angle = product.astype(jnp.float32) * (2.0 * math.pi / length)
    return jnp.stack([jnp.cos(angle), -jnp.sin(angle)], axis=1).astype(jnp.bfloat16)


def y_rows(length, kept, weighted):
    modes = jnp.arange(kept, dtype=jnp.int32)
    places = jnp.arange(length, dtype=jnp.int32)
    angle = (places[:, None] * modes[None, :] % length).astype(jnp.float32) * (
        2.0 * math.pi / length
    )
    cosine = jnp.cos(angle)
    sine = jnp.sin(angle)
    rows = jnp.stack(
        [jnp.stack([cosine, -sine], axis=1), jnp.stack([sine, cosine], axis=1)], axis=0
    )
    if weighted:
        rows = rows * jnp.where(modes == 0, 1.0, 2.0).astype(jnp.float32)
    return rows


def pdot(form, left, right):
    return jnp.einsum(form, left, right, preferred_element_type=jnp.float32)


def padded_block(field):
    return padded_2(field, (("gx", 2), ("gy", 3)), 1)


def forward_chain(field, ytab, factor):
    count_x = lax.axis_size("gx")
    strip_x = lax.axis_index("gx")
    width_x = field.shape[2]
    length_x = width_x * count_x
    positions = strip_x * width_x + jnp.arange(width_x, dtype=jnp.int32)
    modes = kx_values(
        jnp.arange(M1 // count_x * lax.axis_size("gx"), dtype=jnp.int32), length_x, M1
    )
    summed = lax.psum_scatter(
        pdot("msx,lcxy->mslcy", x_table(modes, positions, length_x), field),
        "gx",
        scatter_dimension=0,
        tiled=True,
    )
    spec_x = (summed * factor).astype(jnp.bfloat16)
    spec_x = lax.all_to_all(spec_x, "gy", split_axis=0, concat_axis=4, tiled=True)
    return pdot("mslcy,sytq->mtlcq", spec_x, ytab).astype(jnp.bfloat16)


def inverse_chain(spec, ytab, factor, width_x):
    count_x = lax.axis_size("gx")
    strip_x = lax.axis_index("gx")
    length_x = width_x * count_x
    over_y = pdot("mtldq,tqpy->mpldy", spec, ytab).astype(jnp.bfloat16)
    rows = lax.all_to_all(over_y, "gy", split_axis=4, concat_axis=0, tiled=True)
    positions = strip_x * width_x + jnp.arange(width_x, dtype=jnp.int32)
    piece = lax.all_gather(rows, "gx", axis=0, tiled=True)
    modes = kx_values(jnp.arange(piece.shape[0], dtype=jnp.int32), length_x, M1)
    total = pdot("mpldy,mpx->ldxy", piece, x_table(modes, positions, length_x))
    return (total * factor).astype(jnp.bfloat16)


def mix_modes(spec, weight):
    real_s, imag_s = (spec[:, 0], spec[:, 1])
    real_w, imag_w = (weight[:, :, 0], weight[:, :, 1])
    form = "mlcq,cdmq->mldq"
    real_v = pdot(form, real_s, real_w) - pdot(form, imag_s, imag_w)
    imag_v = pdot(form, real_s, imag_w) + pdot(form, imag_s, real_w)
    return jnp.stack([real_v, imag_v], axis=1).astype(jnp.bfloat16)


def mix_grads(spec, weight, dmixed):
    real_s, imag_s = (spec[:, 0], spec[:, 1])
    real_w, imag_w = (weight[:, :, 0], weight[:, :, 1])
    real_d, imag_d = (dmixed[:, 0], dmixed[:, 1])
    form_w = "mlcq,mldq->cdmq"
    grad_real = pdot(form_w, real_s, real_d) + pdot(form_w, imag_s, imag_d)
    grad_imag = pdot(form_w, real_s, imag_d) - pdot(form_w, imag_s, real_d)
    form_s = "cdmq,mldq->mlcq"
    dreal = pdot(form_s, real_w, real_d) + pdot(form_s, imag_w, imag_d)
    dimag = pdot(form_s, real_w, imag_d) - pdot(form_s, imag_w, real_d)
    grads = jnp.stack([grad_real, grad_imag], axis=2)
    return (grads, jnp.stack([dreal, dimag], axis=1).astype(jnp.bfloat16))


def conv_forward(padded, weight, rows, cols):
    total = jnp.zeros((padded.shape[0], weight.shape[1], rows, cols), jnp.float32)
    for row_tap in range(3):
        for col_tap in range(3):
            window = padded[:, :, row_tap : row_tap + rows, col_tap : col_tap + cols]
            total = total + pdot("dc,lcxy->ldxy", weight[3 * row_tap + col_tap], window)
    return total


def conv_backward(padded, weight, rows, cols):
    total = jnp.zeros((padded.shape[0], weight.shape[2], rows, cols), jnp.float32)
    for row_tap in range(3):
        for col_tap in range(3):
            window = padded[
                :, :, 2 - row_tap : 2 - row_tap + rows, 2 - col_tap : 2 - col_tap + cols
            ]
            total = total + pdot("dc,ldxy->lcxy", weight[3 * row_tap + col_tap], window)
    return total


def body(field_in, spectral_weight, conv_weight, conv_bias, upstream):
    width_x = field_in.shape[2]
    width_y = field_in.shape[3]
    length_y = width_y * lax.axis_size("gy")
    scale = 1.0 / (width_x * lax.axis_size("gx") * length_y)
    plain = y_rows(length_y, M2, False)
    weighted = y_rows(length_y, M2, True)
    fy_table = plain.astype(jnp.bfloat16)
    ay_table = weighted.astype(jnp.bfloat16)
    gy_table = jnp.transpose(weighted, (2, 3, 0, 1)).astype(jnp.bfloat16)
    by_table = jnp.transpose(plain, (2, 3, 0, 1)).astype(jnp.bfloat16)
    spec = forward_chain(field_in, fy_table, 1.0)
    mixed = mix_modes(spec, spectral_weight)
    spectral = inverse_chain(mixed, gy_table, scale, width_x)
    local = conv_forward(padded_block(field_in), conv_weight, width_x, width_y)
    pre = spectral.astype(jnp.float32) + local + conv_bias[None, :, None, None]
    gate = jax.nn.sigmoid(pre)
    activation = pre * gate
    dpre = (upstream.astype(jnp.float32) * gate * (1.0 + pre * (1.0 - gate))).astype(jnp.bfloat16)
    dspec = forward_chain(dpre, ay_table, scale)
    weight_grad, dmix = mix_grads(spec, spectral_weight, dspec)
    dfield = inverse_chain(dmix, by_table, 1.0, width_x)
    back_local = conv_backward(padded_block(dpre), conv_weight, width_x, width_y)
    field_grad = dfield.astype(jnp.float32) + back_local
    return (activation, field_grad, weight_grad)


def solution(mesh):
    return jax.shard_map(
        body,
        mesh=mesh,
        in_specs=(
            P("dp", None, "gx", "gy"),
            P(None, None, None, ("gx", "gy"), None),
            P(),
            P(),
            P("dp", None, "gx", "gy"),
        ),
        out_specs=(
            P("dp", None, "gx", "gy"),
            P("dp", None, "gx", "gy"),
            P("dp", None, None, ("gx", "gy"), None),
        ),
        check_vma=False,
    )
```

profile of v0, /device:TPU:33, one launch (start us, length us, event | category | flops | bytes accessed | tf_op | source)
XLA Modules:
  0.0 457.4 jit_solution(8955305337069914426)
XLA Ops:
  7.5 5.8 %convolution_bitcast_fusion.1 = f32[128,2,1,32,256]{4,0,3,1,2:T(8,128)} fusion(bf16[1,32,64,256]{3,2,1,0:T(8,128)(2,1)} %param.5, bf16[128,1,64]{0,2,1:T(8,128)(2,1)S(1)} %get-tuple-element.48, bf16[128,1,64]{0,2,1:T(8,128)(2,1)S(1)} %get-tuple-element.47), kind=kOutput, calls=%fused_computation.5 | convolution fusion | flops 268500992 | bytes 9469952 | tf_op jit(solution)/shard_map/msx,lcxy->mslcy/dot_general | solution.py:55
  15.2 99.1 %reduce-scatter.3.cloned.1.call-done = f32[8,2,1,32,256]{4,0,3,1,2:T(8,128)} async-done(((f32[128,2,1,32,256]{4,0,3,1,2:T(8,128)}), f32[8,2,1,32,256]{4,0,3,1,2:T(8,128)}) %reduce-scatter.3.cloned.1.call-update) | async-done | bytes 524304 | tf_op jit(solution)/shard_map/reduce_scatter | solution.py:71
  116.1 6.7 %all-to-all-start = ((bf16[8,2,1,32,256]{4,3,1,2,0:T(8,128)(2,1)}), bf16[8,2,1,32,256]{4,3,1,2,0:T(8,128)(2,1)S(1)}, u32[]{:S(2)}, u32[]{:S(2)}) async-start(bf16[8,2,1,32,256]{4,3,1,2,0:T(8,128)(2,1)} %copy.63), calls=%async_computation.1 | async-start | bytes 524288 | tf_op jit(solution)/shard_map/all_to_all | solution.py:78
  122.9 2.1 fusion.104
  125.1 7.6 %all-to-all-done = bf16[8,2,1,32,256]{4,3,1,2,0:T(8,128)(2,1)S(1)} async-done(((bf16[8,2,1,32,256]{4,3,1,2,0:T(8,128)(2,1)}), bf16[8,2,1,32,256]{4,3,1,2,0:T(8,128)(2,1)S(1)}, u32[]{:S(2)}, u32[]{:S(2)}) %all-to-all-start) | async-done | bytes 262176 | tf_op jit(solution)/shard_map/all_to_all | solution.py:78
  135.8 2.1 fusion.26
  140.1 11.9 %all_to_all.66 = bf16[4,2,16384]{2,1,0:T(2,128)(2,1)S(1)} all-to-all(bf16[4,2,16384]{2,1,0:T(2,128)(2,1)S(1)} %reshape.513), channel_id=1, replica_groups=mesh['dp'=4,'gx'=16,'gy'=4] {'gy'}, dimensions={0} | all-to-all | bytes 524288 | tf_op jit(solution)/shard_map/all_to_all | solution.py:87
  155.4 5.6 %collective-permute-start = (bf16[1,32,1,256]{3,1,2,0:T(8,128)(2,1)S(1)}, bf16[1,32,1,256]{3,1,2,0:T(8,128)(2,1)S(1)}, u32[]{:S(2)}, u32[]{:S(2)}) collective-permute-start(bf16[1,32,1,256]{3,1,2,0:T(8,128)(2,1)S(1)} %get-tuple-element.34), channel_id=1, source_target_pairs={{0,4},{4,8},{8,12},{12,16},{16,20},{20,24},{24,28},{28,32},{32,36}... | collective-permute-start | bytes 49160 | tf_op jit(solution)/shard_map/ppermute | solution.py:19
  161.0 2.1 collective-permute-start.1
  163.2 2.1 fusion.92
  171.7 4.9 %collective-permute-start.2 = (bf16[1,32,66,1]{2,1,3,0:T(8,128)(2,1)S(1)}, bf16[1,32,66,1]{2,1,3,0:T(8,128)(2,1)S(1)}, u32[]{:S(2)}, u32[]{:S(2)}) collective-permute-start(bf16[1,32,66,1]{2,1,3,0:T(8,128)(2,1)S(1)} %copy.71), channel_id=1, source_target_pairs={{0,1},{1,2},{2,3},{4,5},{5,6},{6,7},{8,9},{9,10},{10,11},{12,13},{... | collective-permute-start | bytes 12680 | tf_op jit(solution)/shard_map/ppermute | solution.py:19
  193.5 9.3 %all-gather.3.cloned.1.call-done = bf16[128,2,1,32,256]{4,0,1,3,2:T(8,128)(2,1)} async-done(((bf16[8,2,1,32,256]{4,0,1,3,2:T(8,128)(2,1)}), bf16[128,2,1,32,256]{4,0,1,3,2:T(8,128)(2,1)}) %all-gather.3.cloned.1.call-update) | async-done | bytes 4194320 | tf_op jit(solution)/shard_map/all_gather | solution.py:89
  202.8 26.7 %multiply_convert_fusion = (bf16[1,32,64,256]{3,2,1,0:T(8,128)(2,1)S(1)}, f32[1,32,64,256]{3,2,1,0:T(8,128)}) fusion(bf16[1,32,64,256]{3,2,1,0:T(8,128)(2,1)S(1)} %copy-done.7, f32[32]{0:T(128)S(1)} %copy-done.12, f32[64,256,32]{1,2,0:T(8,128)} %fusion.53, f32[64,256,32]{1,2,0:T(8,128)} %fusion.57, f32[64,256,32]{1,2,0:T(8,128)} %fusion.61, ...), kind=kOutput, calls=%fused_computation.32 | convolution fusion | flops 281083904 | bytes 27295872 | tf_op jit(solution)/shard_map/mpldy,mpx->ldxy/dot_general | solution.py:55
  229.4 4.5 convolution_bitcast_fusion
  234.1 98.0 %reduce-scatter.5.cloned.1.call-done = f32[8,2,1,32,256]{4,0,3,1,2:T(8,128)} async-done(((f32[128,2,1,32,256]{4,0,3,1,2:T(8,128)}), f32[8,2,1,32,256]{4,0,3,1,2:T(8,128)}) %reduce-scatter.5.cloned.1.call-update) | async-done | bytes 524304 | tf_op jit(solution)/shard_map/reduce_scatter | solution.py:71
  333.2 17.9 %all_to_all.67 = bf16[8,2,1,32,256]{4,3,1,2,0:T(8,128)(2,1)S(1)} all-to-all(bf16[8,2,1,32,256]{4,3,1,2,0:T(8,128)(2,1)S(1)} %copy.87), channel_id=1, replica_groups=mesh['dp'=4,'gx'=16,'gy'=4] {'gy'}, dimensions={0} | all-to-all | bytes 524288 | tf_op jit(solution)/shard_map/all_to_all | solution.py:78
  354.2 2.6 fusion.30
  359.0 11.5 %all_to_all.68 = bf16[4,2,16384]{2,1,0:T(2,128)(2,1)S(1)} all-to-all(bf16[4,2,16384]{2,1,0:T(2,128)(2,1)S(1)} %reshape.515), channel_id=1, replica_groups=mesh['dp'=4,'gx'=16,'gy'=4] {'gy'}, dimensions={0} | all-to-all | bytes 524288 | tf_op jit(solution)/shard_map/all_to_all | solution.py:87
  373.4 5.0 %collective-permute-start.4 = (bf16[1,32,1,256]{3,2,1,0:T(2,128)(2,1)S(1)}, bf16[1,32,1,256]{3,2,1,0:T(2,128)(2,1)S(1)}, u32[]{:S(2)}, u32[]{:S(2)}) collective-permute-start(bf16[1,32,1,256]{3,2,1,0:T(2,128)(2,1)S(1)} %get-tuple-element.31), channel_id=1, source_target_pairs={{0,4},{4,8},{8,12},{12,16},{16,20},{20,24},{24,28},{28,32},{32,36}... | collective-permute-start | bytes 49160 | tf_op jit(solution)/shard_map/ppermute | solution.py:19
  381.1 3.5 collective-permute-done.5
  388.0 3.8 collective-permute-start.7
  395.2 2.1 fusion.76
  397.3 2.1 fusion.88
  401.8 3.7 pad_maximum_fusion.2
  406.3 2.1 fusion.74
  408.4 2.2 slice_bitcast_fusion.5
  410.5 2.1 fusion.78
  412.7 2.1 fusion.80
  414.7 2.1 fusion.84
  416.8 2.1 fusion.86
  422.2 2.4 pad_maximum_fusion.1
  424.6 25.9 %bitcast_add_fusion = f32[1,32,64,256]{3,2,1,0:T(8,128)} fusion(f32[64,256,32]{1,2,0:T(8,128)} %fusion.74, f32[64,256,32]{1,2,0:T(8,128)} %fusion.76, f32[64,256,32]{1,2,0:T(8,128)} %fusion.78, f32[64,256,32]{1,2,0:T(8,128)} %fusion.80, f32[64,256,32]{1,2,0:T(8,128)S(1)} %fusion.82, f32[64,256,32]{1,2,0:T(8,128)} %fusion.84, f32[64,256,32]{1,2,0:T(8,128)} %fusion.86, ...), kind=kOutput, calls=%fused_computation.8 | convolution fusion | flops 274268160 | bytes 25198592 | tf_op jit(solution)/shard_map/mpldy,mpx->ldxy/dot_general | solution.py:55
  (117 shorter events, 61.2 us)
Async XLA Ops:
  7.2 107.1 %reduce-scatter.3.cloned.1.call-start = ((), (), s32[]{:S(2)}) async-start(), calls=%async_computation.6 | async-start | bytes 8912896 | tf_op jit(solution)/shard_map/reduce_scatter | solution.py:71
  116.1 16.6 %all-to-all-start = ((bf16[8,2,1,32,256]{4,3,1,2,0:T(8,128)(2,1)}), bf16[8,2,1,32,256]{4,3,1,2,0:T(8,128)(2,1)S(1)}, u32[]{:S(2)}, u32[]{:S(2)}) async-start(bf16[8,2,1,32,256]{4,3,1,2,0:T(8,128)(2,1)} %copy.63), calls=%async_computation.1 | async-start | bytes 524288 | tf_op jit(solution)/shard_map/all_to_all | solution.py:78
  122.9 79.9 %all-gather.3.cloned.1.call-start = ((), (), s32[]{:S(2)}) async-start(), calls=%async_computation.7 | async-start | bytes 4456448 | tf_op jit(solution)/shard_map/all_gather | solution.py:89
  125.1 12.8 %copy-start.1 = (f32[1,1024,2,128]{3,1,0,2:T(8,128)}, f32[1,1024,2,128]{3,1,0,2:T(8,128)S(1)}, u32[]{:S(2)}) copy-start(f32[1,1024,2,128]{3,1,0,2:T(8,128)S(1)} %get-tuple-element.35) | copy-start | bytes 3145732
  125.1 12.8 %copy-start.3 = (f32[1,1024,2,128]{3,1,0,2:T(8,128)}, f32[1,1024,2,128]{3,1,0,2:T(8,128)S(1)}, u32[]{:S(2)}) copy-start(f32[1,1024,2,128]{3,1,0,2:T(8,128)S(1)} %get-tuple-element.36) | copy-start | bytes 3145732
  125.1 10.7 %copy-start.5 = (bf16[32,32,2,2,128]{4,3,2,1,0:T(2,128)(2,1)S(1)}, bf16[32,32,2,2,128]{4,3,2,1,0:T(2,128)(2,1)}, u32[]{:S(2)}) copy-start(bf16[32,32,2,2,128]{4,3,2,1,0:T(2,128)(2,1)} %param.6) | copy-start | bytes 3145732
  140.1 14.7 %copy-start = (bf16[1,32,64,256]{3,2,1,0:T(8,128)(2,1)S(1)}, bf16[1,32,64,256]{3,2,1,0:T(8,128)(2,1)}, u32[]{:S(2)}) copy-start(bf16[1,32,64,256]{3,2,1,0:T(8,128)(2,1)} %param.5) | copy-start | bytes 3145732
  152.5 10.7 %copy-start.8 = (bf16[9,32,32]{2,1,0:T(8,128)(2,1)S(1)}, bf16[9,32,32]{2,1,0:T(8,128)(2,1)}, u32[]{:S(2)}) copy-start(bf16[9,32,32]{2,1,0:T(8,128)(2,1)} %param.7) | copy-start | bytes 55300
  154.7 177.3 %reduce-scatter.5.cloned.1.call-start = ((), (), s32[]{:S(2)}) async-start(), calls=%async_computation.8 | async-start | bytes 8912896 | tf_op jit(solution)/shard_map/reduce_scatter | solution.py:71
  155.4 9.9 %collective-permute-start = (bf16[1,32,1,256]{3,1,2,0:T(8,128)(2,1)S(1)}, bf16[1,32,1,256]{3,1,2,0:T(8,128)(2,1)S(1)}, u32[]{:S(2)}, u32[]{:S(2)}) collective-permute-start(bf16[1,32,1,256]{3,1,2,0:T(8,128)(2,1)S(1)} %get-tuple-element.34), channel_id=1, source_target_pairs={{0,4},{4,8},{8,12},{12,16},{16,20},{20,24},{24,28},{28,32},{32,36}... | collective-permute-start | bytes 49160 | tf_op jit(solution)/shard_map/ppermute | solution.py:19
  161.0 6.0 %collective-permute-start.1 = (bf16[1,32,1,256]{3,1,2,0:T(8,128)(2,1)S(1)}, bf16[1,32,1,256]{3,1,2,0:T(8,128)(2,1)S(1)}, u32[]{:S(2)}, u32[]{:S(2)}) collective-permute-start(bf16[1,32,1,256]{3,1,2,0:T(8,128)(2,1)S(1)} %get-tuple-element.33), channel_id=1, source_target_pairs={{4,0},{8,4},{12,8},{16,12},{20,16},{24,20},{28,24},{32,28},{36,32}... | collective-permute-start | bytes 49160 | tf_op jit(solution)/shard_map/ppermute | solution.py:21
  169.7 10.3 %collective-permute-start.3 = (bf16[1,32,66,1]{2,1,3,0:T(8,128)(2,1)S(1)}, bf16[1,32,66,1]{2,1,3,0:T(8,128)(2,1)S(1)}, u32[]{:S(2)}, u32[]{:S(2)}) collective-permute-start(bf16[1,32,66,1]{2,1,3,0:T(8,128)(2,1)S(1)} %copy.76), channel_id=1, source_target_pairs={{1,0},{2,1},{3,2},{5,4},{6,5},{7,6},{9,8},{10,9},{11,10},{13,12},{... | collective-permute-start | bytes 12680 | tf_op jit(solution)/shard_map/ppermute | solution.py:21
  171.7 9.3 %collective-permute-start.2 = (bf16[1,32,66,1]{2,1,3,0:T(8,128)(2,1)S(1)}, bf16[1,32,66,1]{2,1,3,0:T(8,128)(2,1)S(1)}, u32[]{:S(2)}, u32[]{:S(2)}) collective-permute-start(bf16[1,32,66,1]{2,1,3,0:T(8,128)(2,1)S(1)} %copy.71), channel_id=1, source_target_pairs={{0,1},{1,2},{2,3},{4,5},{5,6},{6,7},{8,9},{9,10},{10,11},{12,13},{... | collective-permute-start | bytes 12680 | tf_op jit(solution)/shard_map/ppermute | solution.py:19
  191.5 11.2 %copy-start.7 = (bf16[1,32,64,256]{3,2,1,0:T(8,128)(2,1)S(1)}, bf16[1,32,64,256]{3,2,1,0:T(8,128)(2,1)}, u32[]{:S(2)}) copy-start(bf16[1,32,64,256]{3,2,1,0:T(8,128)(2,1)} %param.9) | copy-start | bytes 3145732
  191.5 11.2 %copy-start.12 = (f32[32]{0:T(128)S(1)}, f32[32]{0:T(128)}, u32[]{:S(2)}) copy-start(f32[32]{0:T(128)} %param.8) | copy-start | bytes 388
  234.0 118.2 %copy-start.2 = (f32[1,1024,2,128]{3,1,0,2:T(8,128)S(1)}, f32[1,1024,2,128]{3,1,0,2:T(8,128)}, u32[]{:S(2)}) copy-start(f32[1,1024,2,128]{3,1,0,2:T(8,128)} %copy-done.1) | copy-start | bytes 3145732
  234.0 118.2 %copy-start.4 = (f32[1,1024,2,128]{3,1,0,2:T(8,128)S(1)}, f32[1,1024,2,128]{3,1,0,2:T(8,128)}, u32[]{:S(2)}) copy-start(f32[1,1024,2,128]{3,1,0,2:T(8,128)} %copy-done.3) | copy-start | bytes 3145732
  234.0 190.6 %all-gather.5.cloned.1.call-start = ((), (), s32[]{:S(2)}) async-start(), calls=%async_computation.9 | async-start | bytes 4456448 | tf_op jit(solution)/shard_map/all_gather | solution.py:89
  352.2 2.0 copy-start.6
  359.0 14.3 %copy-start.9 = (f32[2,128,32]{1,2,0:T(8,128)S(1)}, f32[2,128,32]{1,2,0:T(8,128)}, u32[]{:S(2)}) copy-start(f32[2,128,32]{1,2,0:T(8,128)} %get-tuple-element.43) | copy-start | bytes 98308
  373.4 7.7 %collective-permute-start.4 = (bf16[1,32,1,256]{3,2,1,0:T(2,128)(2,1)S(1)}, bf16[1,32,1,256]{3,2,1,0:T(2,128)(2,1)S(1)}, u32[]{:S(2)}, u32[]{:S(2)}) collective-permute-start(bf16[1,32,1,256]{3,2,1,0:T(2,128)(2,1)S(1)} %get-tuple-element.31), channel_id=1, source_target_pairs={{0,4},{4,8},{8,12},{12,16},{16,20},{20,24},{24,28},{28,32},{32,36}... | collective-permute-start | bytes 49160 | tf_op jit(solution)/shard_map/ppermute | solution.py:19
  378.5 6.1 %collective-permute-start.5 = (bf16[1,32,1,256]{3,2,1,0:T(2,128)(2,1)S(1)}, bf16[1,32,1,256]{3,2,1,0:T(2,128)(2,1)S(1)}, u32[]{:S(2)}, u32[]{:S(2)}) collective-permute-start(bf16[1,32,1,256]{3,2,1,0:T(2,128)(2,1)S(1)} %get-tuple-element.32), channel_id=1, source_target_pairs={{4,0},{8,4},{12,8},{16,12},{20,16},{24,20},{28,24},{32,28},{36,32}... | collective-permute-start | bytes 49160 | tf_op jit(solution)/shard_map/ppermute | solution.py:21
  388.0 11.5 %collective-permute-start.7 = (bf16[1,32,66,1]{2,1,3,0:T(8,128)(2,1)S(1)}, bf16[1,32,66,1]{2,1,3,0:T(8,128)(2,1)S(1)}, u32[]{:S(2)}, u32[]{:S(2)}) collective-permute-start(bf16[1,32,66,1]{2,1,3,0:T(8,128)(2,1)S(1)} %copy.100), channel_id=1, source_target_pairs={{0,1},{1,2},{2,3},{4,5},{5,6},{6,7},{8,9},{9,10},{10,11},{12,13},{... | collective-permute-start | bytes 12680 | tf_op jit(solution)/shard_map/ppermute | solution.py:19
  393.2 7.4 %collective-permute-start.6 = (bf16[1,32,66,1]{2,1,3,0:T(8,128)(2,1)S(1)}, bf16[1,32,66,1]{2,1,3,0:T(8,128)(2,1)S(1)}, u32[]{:S(2)}, u32[]{:S(2)}) collective-permute-start(bf16[1,32,66,1]{2,1,3,0:T(8,128)(2,1)S(1)} %copy.92), channel_id=1, source_target_pairs={{1,0},{2,1},{3,2},{5,4},{6,5},{7,6},{9,8},{10,9},{11,10},{13,12},{... | collective-permute-start | bytes 12680 | tf_op jit(solution)/shard_map/ppermute | solution.py:21
  418.9 2.1 copy-start.11
  418.9 2.1 copy-start.10
Sparse Core Ops, SparseCore 0:
  13.4 100.8 reduce-scatter.2
  154.8 47.8 all-gather.2
  234.1 97.9 reduce-scatter.4
  373.4 46.9 all-gather.4
where the time goes:
time: 466 us; the launch traced here: 457 us
  waiting for transfers between devices  219 us (47%)
  matrix products  99.8 us (21%)
  blocking collectives  41.3 us (9%)
  starting transfers between devices  32.9 us (7%)
  local copies, waits for them, and re-layouts  28.8 us (6%)
  other arithmetic  21.3 us (5%)
  between operations  14.7 us (3%)
    reduce_scatter x2, waiting for transfers between devices, forward_chain(): lax.psum_scatter(pdot('msx,lcxy->mslcy', x_table(modes, positions, length...  197 us
    dot_general x26, matrix products, pdot(): return jnp.einsum(form, left, right, preferred_element_type=jnp.float32)  99.8 us
    all_to_all x2, blocking collectives, inverse_chain(): rows = lax.all_to_all(over_y, 'gy', split_axis=4, concat_axis=0, tiled=True)  23.4 us
    ppermute x4, starting transfers between devices, padded_2(): lax.ppermute(tail, axis, [(i, (i + 1) % count) for i in range(ends)])  19.4 us
    all_to_all x1, blocking collectives, forward_chain(): lax.all_to_all(spec_x, 'gy', split_axis=0, concat_axis=4, tiled=True)  17.9 us
  transfers between devices with their start and end apart: 13, of which 6 were waited for; matrix products, arithmetic and copies ran while one was open for 14% of the time, Pallas kernels for 0%

commit v1 on v0

--- a/solution.py
+++ b/solution.py
@@ -86,7 +86,11 @@
     over_y = pdot("mtldq,tqpy->mpldy", spec, ytab).astype(jnp.bfloat16)
     rows = lax.all_to_all(over_y, "gy", split_axis=4, concat_axis=0, tiled=True)
     positions = strip_x * width_x + jnp.arange(width_x, dtype=jnp.int32)
-    piece = lax.all_gather(rows, "gx", axis=0, tiled=True)
+    upper = jax.lax.axis_size("gx")
+    y = jax.lax.all_to_all(
+        jnp.stack([rows] * upper, axis=0), axis_name="gx", split_axis=0, concat_axis=0
+    )
+    piece = jnp.concatenate(y, axis=0)
     modes = kx_values(jnp.arange(piece.shape[0], dtype=jnp.int32), length_x, M1)
     total = pdot("mpldy,mpx->ldxy", piece, x_table(modes, positions, length_x))
     return (total * factor).astype(jnp.bfloat16)

time: 466 us -> 552 us (1.18)
  the two profiles are of different devices: /device:TPU:33 before, /device:TPU:1 now
where the time goes in v1:
time: 552 us; the launch traced here: 543 us
  waiting for transfers between devices  289 us (52%)
  matrix products  99.8 us (18%)
  starting transfers between devices  47.2 us (9%)
  blocking collectives  39.3 us (7%)
  local copies, waits for them, and re-layouts  30.7 us (6%)
  other arithmetic  21.2 us (4%)
  between operations  15 us (3%)
    reduce_scatter x2, waiting for transfers between devices, forward_chain(): lax.psum_scatter(pdot('msx,lcxy->mslcy', x_table(modes, positions, length...  198 us
    dot_general x26, matrix products, pdot(): return jnp.einsum(form, left, right, preferred_element_type=jnp.float32)  99.8 us
    ppermute x4, waiting for transfers between devices, padded_2(): lax.ppermute(tail, axis, [(i, (i + 1) % count) for i in range(ends)])  79.7 us
    all_to_all x2, blocking collectives, inverse_chain(): rows = lax.all_to_all(over_y, 'gy', split_axis=4, concat_axis=0, tiled=True)  23.8 us
    all_to_all x2, starting transfers between devices, inverse_chain(): jax.lax.all_to_all(jnp.stack([rows] * upper, axis=0), axis_name='gx', spl...  17.9 us
    ppermute x4, starting transfers between devices, padded_2(): lax.ppermute(tail, axis, [(i, (i + 1) % count) for i in range(ends)])  16.8 us
    all_to_all x1, blocking collectives, forward_chain(): lax.all_to_all(spec_x, 'gy', split_axis=0, concat_axis=4, tiled=True)  15.5 us
  transfers between devices with their start and end apart: 13, of which 7 were waited for; matrix products, arithmetic and copies ran while one was open for 11% of the time, Pallas kernels for 0%

profile of v1, /device:TPU:1, one launch (start us, length us, event | category | flops | bytes accessed | tf_op | source)
XLA Modules:
  0.0 542.5 jit_solution(702526747833545362)
XLA Ops:
  7.5 5.7 %convolution_bitcast_fusion.1 = f32[128,2,1,32,256]{4,0,3,1,2:T(8,128)} fusion(bf16[1,32,64,256]{3,2,1,0:T(8,128)(2,1)} %param.5, bf16[128,1,64]{0,2,1:T(8,128)(2,1)S(1)} %get-tuple-element.48, bf16[128,1,64]{0,2,1:T(8,128)(2,1)S(1)} %get-tuple-element.47), kind=kOutput, calls=%fused_computation.7 | convolution fusion | flops 268500992 | bytes 9469952 | tf_op jit(solution)/shard_map/msx,lcxy->mslcy/dot_general | solution.py:55
  15.2 100.7 %reduce-scatter.3.cloned.1.call-done = f32[8,2,1,32,256]{4,0,3,1,2:T(8,128)} async-done(((f32[128,2,1,32,256]{4,0,3,1,2:T(8,128)}), f32[8,2,1,32,256]{4,0,3,1,2:T(8,128)}) %reduce-scatter.3.cloned.1.call-update) | async-done | bytes 524304 | tf_op jit(solution)/shard_map/reduce_scatter | solution.py:71
  117.7 5.8 %all-to-all-start = ((bf16[8,2,1,32,256]{4,3,1,2,0:T(8,128)(2,1)}), bf16[8,2,1,32,256]{4,3,1,2,0:T(8,128)(2,1)S(1)}, u32[]{:S(2)}, u32[]{:S(2)}) async-start(bf16[8,2,1,32,256]{4,3,1,2,0:T(8,128)(2,1)} %copy.185), calls=%async_computation.1 | async-start | bytes 524288 | tf_op jit(solution)/shard_map/all_to_all | solution.py:78
  125.8 7.2 %all-to-all-done = bf16[8,2,1,32,256]{4,3,1,2,0:T(8,128)(2,1)S(1)} async-done(((bf16[8,2,1,32,256]{4,3,1,2,0:T(8,128)(2,1)}), bf16[8,2,1,32,256]{4,3,1,2,0:T(8,128)(2,1)S(1)}, u32[]{:S(2)}, u32[]{:S(2)}) %all-to-all-start) | async-done | bytes 262176 | tf_op jit(solution)/shard_map/all_to_all | solution.py:78
  140.3 11.8 %all_to_all.70 = bf16[4,2,16384]{2,1,0:T(2,128)(2,1)S(1)} all-to-all(bf16[4,2,16384]{2,1,0:T(2,128)(2,1)S(1)} %reshape.527), channel_id=1, replica_groups=mesh['dp'=4,'gx'=16,'gy'=4] {'gy'}, dimensions={0} | all-to-all | bytes 524288 | tf_op jit(solution)/shard_map/all_to_all | solution.py:87
  154.3 2.4 stack.39
  156.7 9.0 %all-to-all-start.2 = ((bf16[16,8,2,1,32,256]{5,1,2,4,3,0:T(8,128)(2,1)}), bf16[16,8,2,1,32,256]{5,1,2,4,3,0:T(8,128)(2,1)}, u32[]{:S(2)}, u32[]{:S(2)}) async-start(bf16[16,8,2,1,32,256]{5,1,2,4,3,0:T(8,128)(2,1)} %stack.39), calls=%async_computation.3 | async-start | bytes 8388608 | tf_op jit(solution)/shard_map/all_to_all | solution.py:90
  166.3 3.5 collective-permute-start
  169.9 2.1 collective-permute-start.1
  172.0 2.1 fusion.94
  174.1 38.6 %collective-permute-done = bf16[1,32,1,256]{3,1,2,0:T(8,128)(2,1)S(1)} collective-permute-done((bf16[1,32,1,256]{3,1,2,0:T(8,128)(2,1)S(1)}, bf16[1,32,1,256]{3,1,2,0:T(8,128)(2,1)S(1)}, u32[]{:S(2)}, u32[]{:S(2)}) %collective-permute-start) | collective-permute-done | bytes 16416 | tf_op jit(solution)/shard_map/ppermute | solution.py:19
  218.0 4.9 collective-permute-start.2
  239.9 26.5 %multiply_convert_fusion = (bf16[1,32,64,256]{3,2,1,0:T(8,128)(2,1)S(1)}, f32[1,32,64,256]{3,2,1,0:T(8,128)}) fusion(bf16[1,32,64,256]{3,2,1,0:T(8,128)(2,1)S(1)} %copy-done.7, f32[32]{0:T(128)S(1)} %copy-done.12, f32[64,256,32]{1,2,0:T(8,128)} %fusion.55, f32[64,256,32]{1,2,0:T(8,128)} %fusion.59, f32[64,256,32]{1,2,0:T(8,128)} %fusion.63, ...), kind=kOutput, calls=%fused_computation.34 | convolution fusion | flops 281083904 | bytes 27295872 | tf_op jit(solution)/shard_map/mpldy,mpx->ldxy/dot_general | solution.py:55
  266.4 4.5 convolution_bitcast_fusion
  271.0 97.5 %reduce-scatter.5.cloned.1.call-done = f32[8,2,1,32,256]{4,0,3,1,2:T(8,128)} async-done(((f32[128,2,1,32,256]{4,0,3,1,2:T(8,128)}), f32[8,2,1,32,256]{4,0,3,1,2:T(8,128)}) %reduce-scatter.5.cloned.1.call-update) | async-done | bytes 524304 | tf_op jit(solution)/shard_map/reduce_scatter | solution.py:71
  369.6 15.5 %all_to_all.71 = bf16[8,2,1,32,256]{4,3,1,2,0:T(8,128)(2,1)S(1)} all-to-all(bf16[8,2,1,32,256]{4,3,1,2,0:T(8,128)(2,1)S(1)} %copy.212), channel_id=1, replica_groups=mesh['dp'=4,'gx'=16,'gy'=4] {'gy'}, dimensions={0} | all-to-all | bytes 524288 | tf_op jit(solution)/shard_map/all_to_all | solution.py:78
  388.3 2.6 fusion.32
  393.0 12.0 %all_to_all.72 = bf16[4,2,16384]{2,1,0:T(2,128)(2,1)S(1)} all-to-all(bf16[4,2,16384]{2,1,0:T(2,128)(2,1)S(1)} %reshape.529), channel_id=1, replica_groups=mesh['dp'=4,'gx'=16,'gy'=4] {'gy'}, dimensions={0} | all-to-all | bytes 524288 | tf_op jit(solution)/shard_map/all_to_all | solution.py:87
  407.2 2.4 stack.42
  409.6 8.8 %all-to-all-start.5 = ((bf16[16,8,2,1,32,256]{5,1,2,4,3,0:T(8,128)(2,1)}), bf16[16,8,2,1,32,256]{5,1,2,4,3,0:T(8,128)(2,1)}, u32[]{:S(2)}, u32[]{:S(2)}) async-start(bf16[16,8,2,1,32,256]{5,1,2,4,3,0:T(8,128)(2,1)} %stack.42), calls=%async_computation.7 | async-start | bytes 8388608 | tf_op jit(solution)/shard_map/all_to_all | solution.py:90
  418.6 3.5 collective-permute-start.4
  424.8 41.1 %collective-permute-done.4 = bf16[1,32,1,256]{3,2,1,0:T(2,128)(2,1)S(1)} collective-permute-done((bf16[1,32,1,256]{3,2,1,0:T(2,128)(2,1)S(1)}, bf16[1,32,1,256]{3,2,1,0:T(2,128)(2,1)S(1)}, u32[]{:S(2)}, u32[]{:S(2)}) %collective-permute-start.4) | collective-permute-done | bytes 16416 | tf_op jit(solution)/shard_map/ppermute | solution.py:19
  465.9 2.4 collective-permute-done.5
  474.3 4.9 collective-permute-start.7
  482.0 2.1 fusion.90
  486.5 3.7 pad_maximum_fusion.2
  490.9 2.1 fusion.76
  493.1 2.2 slice_bitcast_fusion.5
  495.3 2.1 fusion.80
  503.5 2.1 fusion.92
  506.9 2.4 pad_maximum_fusion.1
  509.3 25.9 %bitcast_add_fusion = f32[1,32,64,256]{3,2,1,0:T(8,128)} fusion(f32[64,256,32]{1,2,0:T(8,128)} %fusion.76, f32[64,256,32]{1,2,0:T(8,128)} %fusion.78, f32[64,256,32]{1,2,0:T(8,128)} %fusion.80, f32[64,256,32]{1,2,0:T(8,128)} %fusion.82, f32[64,256,32]{1,2,0:T(8,128)S(1)} %fusion.84, f32[64,256,32]{1,2,0:T(8,128)} %fusion.86, f32[64,256,32]{1,2,0:T(8,128)} %fusion.88, ...), kind=kOutput, calls=%fused_computation.10 | convolution fusion | flops 274268160 | bytes 25198592 | tf_op jit(solution)/shard_map/mpldy,mpx->ldxy/dot_general | solution.py:55
  (119 shorter events, 69.2 us)
Async XLA Ops:
  7.2 108.7 %reduce-scatter.3.cloned.1.call-start = ((), (), s32[]{:S(2)}) async-start(), calls=%async_computation.8 | async-start | bytes 8912896 | tf_op jit(solution)/shard_map/reduce_scatter | solution.py:71
  117.7 15.3 %all-to-all-start = ((bf16[8,2,1,32,256]{4,3,1,2,0:T(8,128)(2,1)}), bf16[8,2,1,32,256]{4,3,1,2,0:T(8,128)(2,1)S(1)}, u32[]{:S(2)}, u32[]{:S(2)}) async-start(bf16[8,2,1,32,256]{4,3,1,2,0:T(8,128)(2,1)} %copy.185), calls=%async_computation.1 | async-start | bytes 524288 | tf_op jit(solution)/shard_map/all_to_all | solution.py:78
  125.8 12.3 %copy-start.1 = (f32[1,1024,2,128]{3,1,0,2:T(8,128)}, f32[1,1024,2,128]{3,1,0,2:T(8,128)S(1)}, u32[]{:S(2)}) copy-start(f32[1,1024,2,128]{3,1,0,2:T(8,128)S(1)} %get-tuple-element.35) | copy-start | bytes 3145732
  125.8 12.3 %copy-start.3 = (f32[1,1024,2,128]{3,1,0,2:T(8,128)}, f32[1,1024,2,128]{3,1,0,2:T(8,128)S(1)}, u32[]{:S(2)}) copy-start(f32[1,1024,2,128]{3,1,0,2:T(8,128)S(1)} %get-tuple-element.36) | copy-start | bytes 3145732
  125.8 10.2 %copy-start.5 = (bf16[32,32,2,2,128]{4,3,2,1,0:T(2,128)(2,1)S(1)}, bf16[32,32,2,2,128]{4,3,2,1,0:T(2,128)(2,1)}, u32[]{:S(2)}) copy-start(bf16[32,32,2,2,128]{4,3,2,1,0:T(2,128)(2,1)} %param.6) | copy-start | bytes 3145732
  156.7 9.1 %copy-start = (bf16[1,32,64,256]{3,2,1,0:T(8,128)(2,1)S(1)}, bf16[1,32,64,256]{3,2,1,0:T(8,128)(2,1)}, u32[]{:S(2)}) copy-start(bf16[1,32,64,256]{3,2,1,0:T(8,128)(2,1)} %param.5) | copy-start | bytes 3145732
  156.7 83.2 %all-to-all-start.2 = ((bf16[16,8,2,1,32,256]{5,1,2,4,3,0:T(8,128)(2,1)}), bf16[16,8,2,1,32,256]{5,1,2,4,3,0:T(8,128)(2,1)}, u32[]{:S(2)}, u32[]{:S(2)}) async-start(bf16[16,8,2,1,32,256]{5,1,2,4,3,0:T(8,128)(2,1)} %stack.39), calls=%async_computation.3 | async-start | bytes 8388608 | tf_op jit(solution)/shard_map/all_to_all | solution.py:90
  165.7 6.4 %copy-start.8 = (bf16[9,32,32]{2,1,0:T(8,128)(2,1)S(1)}, bf16[9,32,32]{2,1,0:T(8,128)(2,1)}, u32[]{:S(2)}) copy-start(bf16[9,32,32]{2,1,0:T(8,128)(2,1)} %param.7) | copy-start | bytes 55300
  165.7 202.8 %reduce-scatter.5.cloned.1.call-start = ((), (), s32[]{:S(2)}) async-start(), calls=%async_computation.9 | async-start | bytes 8912896 | tf_op jit(solution)/shard_map/reduce_scatter | solution.py:71
  166.3 46.4 %collective-permute-start = (bf16[1,32,1,256]{3,1,2,0:T(8,128)(2,1)S(1)}, bf16[1,32,1,256]{3,1,2,0:T(8,128)(2,1)S(1)}, u32[]{:S(2)}, u32[]{:S(2)}) collective-permute-start(bf16[1,32,1,256]{3,1,2,0:T(8,128)(2,1)S(1)} %get-tuple-element.34), channel_id=1, source_target_pairs={{0,4},{4,8},{8,12},{12,16},{16,20},{20,24},{24,28},{28,32},{32,36}... | collective-permute-start | bytes 49160 | tf_op jit(solution)/shard_map/ppermute | solution.py:19
  169.9 45.2 %collective-permute-start.1 = (bf16[1,32,1,256]{3,1,2,0:T(8,128)(2,1)S(1)}, bf16[1,32,1,256]{3,1,2,0:T(8,128)(2,1)S(1)}, u32[]{:S(2)}, u32[]{:S(2)}) collective-permute-start(bf16[1,32,1,256]{3,1,2,0:T(8,128)(2,1)S(1)} %get-tuple-element.33), channel_id=1, source_target_pairs={{4,0},{8,4},{12,8},{16,12},{20,16},{24,20},{28,24},{32,28},{36,32}... | collective-permute-start | bytes 49160 | tf_op jit(solution)/shard_map/ppermute | solution.py:21
  216.1 10.3 %collective-permute-start.3 = (bf16[1,32,66,1]{2,1,3,0:T(8,128)(2,1)S(1)}, bf16[1,32,66,1]{2,1,3,0:T(8,128)(2,1)S(1)}, u32[]{:S(2)}, u32[]{:S(2)}) collective-permute-start(bf16[1,32,66,1]{2,1,3,0:T(8,128)(2,1)S(1)} %copy.201), channel_id=1, source_target_pairs={{1,0},{2,1},{3,2},{5,4},{6,5},{7,6},{9,8},{10,9},{11,10},{13,12},{... | collective-permute-start | bytes 12680 | tf_op jit(solution)/shard_map/ppermute | solution.py:21
  218.0 9.3 %collective-permute-start.2 = (bf16[1,32,66,1]{2,1,3,0:T(8,128)(2,1)S(1)}, bf16[1,32,66,1]{2,1,3,0:T(8,128)(2,1)S(1)}, u32[]{:S(2)}, u32[]{:S(2)}) collective-permute-start(bf16[1,32,66,1]{2,1,3,0:T(8,128)(2,1)S(1)} %copy.196), channel_id=1, source_target_pairs={{0,1},{1,2},{2,3},{4,5},{5,6},{6,7},{8,9},{9,10},{10,11},{12,13},{... | collective-permute-start | bytes 12680 | tf_op jit(solution)/shard_map/ppermute | solution.py:19
  237.9 2.0 copy-start.7
  237.9 2.0 copy-start.12
  271.0 115.2 %copy-start.2 = (f32[1,1024,2,128]{3,1,0,2:T(8,128)S(1)}, f32[1,1024,2,128]{3,1,0,2:T(8,128)}, u32[]{:S(2)}) copy-start(f32[1,1024,2,128]{3,1,0,2:T(8,128)} %copy-done.1) | copy-start | bytes 3145732
  271.0 115.2 %copy-start.4 = (f32[1,1024,2,128]{3,1,0,2:T(8,128)S(1)}, f32[1,1024,2,128]{3,1,0,2:T(8,128)}, u32[]{:S(2)}) copy-start(f32[1,1024,2,128]{3,1,0,2:T(8,128)} %copy-done.3) | copy-start | bytes 3145732
  386.2 2.0 copy-start.6
  409.6 8.9 %copy-start.9 = (f32[2,128,32]{1,2,0:T(8,128)S(1)}, f32[2,128,32]{1,2,0:T(8,128)}, u32[]{:S(2)}) copy-start(f32[2,128,32]{1,2,0:T(8,128)} %get-tuple-element.43) | copy-start | bytes 98308
  409.6 99.7 %all-to-all-start.5 = ((bf16[16,8,2,1,32,256]{5,1,2,4,3,0:T(8,128)(2,1)}), bf16[16,8,2,1,32,256]{5,1,2,4,3,0:T(8,128)(2,1)}, u32[]{:S(2)}, u32[]{:S(2)}) async-start(bf16[16,8,2,1,32,256]{5,1,2,4,3,0:T(8,128)(2,1)} %stack.42), calls=%async_computation.7 | async-start | bytes 8388608 | tf_op jit(solution)/shard_map/all_to_all | solution.py:90
  418.6 47.3 %collective-permute-start.4 = (bf16[1,32,1,256]{3,2,1,0:T(2,128)(2,1)S(1)}, bf16[1,32,1,256]{3,2,1,0:T(2,128)(2,1)S(1)}, u32[]{:S(2)}, u32[]{:S(2)}) collective-permute-start(bf16[1,32,1,256]{3,2,1,0:T(2,128)(2,1)S(1)} %get-tuple-element.31), channel_id=1, source_target_pairs={{0,4},{4,8},{8,12},{12,16},{16,20},{20,24},{24,28},{28,32},{32,36}... | collective-permute-start | bytes 49160 | tf_op jit(solution)/shard_map/ppermute | solution.py:19
  422.1 46.1 %collective-permute-start.5 = (bf16[1,32,1,256]{3,2,1,0:T(2,128)(2,1)S(1)}, bf16[1,32,1,256]{3,2,1,0:T(2,128)(2,1)S(1)}, u32[]{:S(2)}, u32[]{:S(2)}) collective-permute-start(bf16[1,32,1,256]{3,2,1,0:T(2,128)(2,1)S(1)} %get-tuple-element.32), channel_id=1, source_target_pairs={{4,0},{8,4},{12,8},{16,12},{20,16},{24,20},{28,24},{32,28},{36,32}... | collective-permute-start | bytes 49160 | tf_op jit(solution)/shard_map/ppermute | solution.py:21
  471.6 12.5 %collective-permute-start.6 = (bf16[1,32,66,1]{2,1,3,0:T(8,128)(2,1)S(1)}, bf16[1,32,66,1]{2,1,3,0:T(8,128)(2,1)S(1)}, u32[]{:S(2)}, u32[]{:S(2)}) collective-permute-start(bf16[1,32,66,1]{2,1,3,0:T(8,128)(2,1)S(1)} %copy.220), channel_id=1, source_target_pairs={{1,0},{2,1},{3,2},{5,4},{6,5},{7,6},{9,8},{10,9},{11,10},{13,12},{... | collective-permute-start | bytes 12680 | tf_op jit(solution)/shard_map/ppermute | solution.py:21
  474.3 11.0 %collective-permute-start.7 = (bf16[1,32,66,1]{2,1,3,0:T(8,128)(2,1)S(1)}, bf16[1,32,66,1]{2,1,3,0:T(8,128)(2,1)S(1)}, u32[]{:S(2)}, u32[]{:S(2)}) collective-permute-start(bf16[1,32,66,1]{2,1,3,0:T(8,128)(2,1)S(1)} %copy.228), channel_id=1, source_target_pairs={{0,1},{1,2},{2,3},{4,5},{5,6},{6,7},{8,9},{9,10},{10,11},{12,13},{... | collective-permute-start | bytes 12680 | tf_op jit(solution)/shard_map/ppermute | solution.py:19
  503.5 2.1 copy-start.11
  503.5 2.1 copy-start.10
Sparse Core Ops, SparseCore 0:
  13.3 102.5 reduce-scatter.2
  271.1 97.3 reduce-scatter.4
